TPU v7x, 32 devices: a whole 2x2x4 slice. The times are simulated.
32 devices in a mesh: gx: 8 (over z, x), gy: 2 (over y), pa: 2 (over core).
Axes of the slice: x: 2, y: 2, z: 4, core: 2. Of those that a mesh axis runs over, the one named last changes fastest.
Arguments:
- leaf_maps: bfloat16 [8, 2, 2, 1024, 1024], P('gx', 'gy', None, 'pa'), may hold values from -0.125 to 0.125
- face_index: int32 [8, 2, 1024], P('gx', 'gy'), may hold values from 0 to 1023, each once within a row
- order_x: int32 [4, 2], replicated, may hold values from 0 to 1
- order_y: int32 [4, 1], replicated, may hold values from 0 to 1
- traces: float32 [8, 2, 2, 1024], P('gx', 'gy'), may hold values from -6 to 6
Outputs:
- merged_map: bfloat16 [8, 2, 2, 2, 128, 1024], P('gx', 'gy', 'pa')
- outgoing: float32 [8, 2, 2, 2, 128], P('gx', 'gy', 'pa')
Inputs may be any that keep to these rules, and one draw needn't show every extreme that they name: `face_index`: each row is a permutation of 0 to 1023.
All inputs are finite; a program needn't handle non-finite values.
Results may differ from a plain program's by a relative error of at most 0.0058.
Values may be sent and summed in bfloat16 or wider, within the bound.
A program may use at most 64 MiB of HBM per device.

v0:
```python
import jax
import jax.numpy as jnp
from jax import lax
from jax.sharding import PartitionSpec as P


def from_partner(value, axis, apart):
    mask = 2**apart
    pairs = [(source, source ^ mask) for source in range(lax.axis_size(axis))]
    return lax.ppermute(value, axis, pairs)


def complex_rows(left_block, right_block):
    real_part = jnp.dot(
        left_block[0], right_block[0], preferred_element_type=jnp.float32
    ) - jnp.dot(left_block[1], right_block[1], preferred_element_type=jnp.float32)
    imag_part = jnp.dot(
        left_block[0], right_block[1], preferred_element_type=jnp.float32
    ) + jnp.dot(left_block[1], right_block[0], preferred_element_type=jnp.float32)
    return (real_part, imag_part)


def folder(left_rows, segment):
    real_part, imag_part = complex_rows(left_rows, segment)
    return (real_part, imag_part)


def per_device(leaf_maps, face_index, order_x, order_y, traces):
    own_panel = jnp.take(leaf_maps[0, 0], face_index[0, 0], axis=2)
    panel_rows = own_panel.shape[1]
    width = own_panel.shape[2]
    half_rows = panel_rows // 2
    quarter = panel_rows // 4
    half_index = lax.axis_index("gx") % 2
    vert_index = lax.axis_index("gy") % 2
    pair_index = lax.axis_index("gx") // 2
    column_index = lax.axis_index("gy")
    first_bit = order_x[pair_index, column_index]
    sibling = from_partner(own_panel, "gx", 0)
    right_panel = jnp.where(half_index == first_bit, own_panel, sibling)
    left_panel = jnp.where(half_index == first_bit, sibling, own_panel)
    left_rows = lax.dynamic_slice_in_dim(left_panel, half_index * half_rows, half_rows, 1)
    blocks = lax.all_to_all(left_rows, "pa", split_axis=2, concat_axis=1, tiled=True)
    real_part, imag_part = complex_rows(blocks, right_panel)
    summed = lax.psum_scatter(
        jnp.concatenate([real_part, imag_part], axis=1), "pa", scatter_dimension=0, tiled=True
    )
    real_one = summed[:, :width]
    imag_one = summed[:, width:]
    merged_one = jnp.stack([real_one, imag_one]).astype(jnp.bfloat16)
    second_bit = order_y[pair_index, column_index // 2]
    other_box = from_partner(merged_one, "gy", 0)
    right_two = jnp.where(vert_index == second_bit, merged_one, other_box)
    left_two = jnp.where(vert_index == second_bit, other_box, merged_one)
    left_rows_two = lax.dynamic_slice_in_dim(left_two, vert_index * quarter, quarter, 1)
    other_half = from_partner(right_two, "gx", 0)
    first_part = jnp.where(half_index == 0, right_two, other_half)
    second_part = jnp.where(half_index == 0, other_half, right_two)
    full_panel = jnp.concatenate([first_part, second_part], axis=1)
    real_two, imag_two = folder(left_rows_two, lax.all_gather(full_panel, "pa", axis=1, tiled=True))
    merged_two = jnp.stack([real_two, imag_two]).astype(jnp.bfloat16)
    trace_sum = traces[0, 0] + from_partner(traces[0, 0], "gx", 0)
    trace_sum = trace_sum + from_partner(trace_sum, "gy", 0)
    wide = merged_two.astype(jnp.float32)
    highest = lax.Precision.HIGHEST
    real_out = jnp.dot(wide[0], trace_sum[0], precision=highest) - jnp.dot(
        wide[1], trace_sum[1], precision=highest
    )
    imag_out = jnp.dot(wide[0], trace_sum[1], precision=highest) + jnp.dot(
        wide[1], trace_sum[0], precision=highest
    )
    outgoing = jnp.stack([real_out, imag_out]).reshape(1, 1, 1, 2, quarter)
    return (merged_two.reshape(1, 1, 1, 2, quarter, width), outgoing)


def solution(mesh):
    placed = (
        P("gx", "gy", None, "pa", None),
        P("gx", "gy", None),
        P(),
        P(),
        P("gx", "gy", None, None),
    )
    return jax.shard_map(
        per_device,
        mesh=mesh,
        in_specs=placed,
        out_specs=(P("gx", "gy", "pa", None, None, None), P("gx", "gy", "pa", None, None)),
        check_vma=False,
    )
```

profile of v0, /device:TPU:0, one launch (start us, length us, event | category | flops | bytes accessed | tf_op | source)
XLA Modules:
  0.0 207.1 jit_solution(6228542808558593444)
XLA Ops:
  7.2 6.2 %copy.9 = bf16[1,1,2,512,1024]{3,2,4,1,0:T(2,128)(2,1)} copy(bf16[1,1,2,512,1024]{4,3,2,1,0:T(8,128)(2,1)} %param.5) | data formatting | bytes 4194304 | tf_op args[0]
  13.4 7.5 %gather_fusion = bf16[1024,2,512]{2,1,0:T(2,128)(2,1)S(1)} fusion(bf16[2,512,1024]{1,0,2:T(2,128)(2,1)} %bitcast.99, s32[1024]{0:T(1024)S(1)} %broadcast_clamp_fusion), kind=kCustom, calls=%fused_computation | custom fusion | bytes 4198400 | tf_op jit(solution)/shard_map/jit(_take)/gather | solution.py:29
  20.9 4.6 %fusion = bf16[2,512,1024]{1,0,2:T(2,128)(2,1)} fusion(bf16[1024,2,512]{2,1,0:T(2,128)(2,1)S(1)} %gather_fusion, pred[1024]{0:T(1024)(128)(4,1)S(1)} %compare_and_fusion), kind=kLoop, calls=%fused_computation.7 | loop fusion | flops 1048576 | bytes 4195328 | tf_op jit(solution)/shard_map/jit(_take)/select_n | solution.py:29
  25.5 3.0 %collective-permute-start = (bf16[2,512,1024]{1,0,2:T(2,128)(2,1)}, bf16[2,512,1024]{1,0,2:T(2,128)(2,1)}, u32[]{:S(2)}, u32[]{:S(2)}) collective-permute-start(bf16[2,512,1024]{1,0,2:T(2,128)(2,1)} %fusion), channel_id=1, source_target_pairs={{0,4},{4,0},{8,12},{12,8},{16,20},{20,16},{24,28},{28,24},{1,5},{5... | collective-permute-start | bytes 6291464 | tf_op jit(solution)/shard_map/ppermute | solution.py:10
  28.5 0.6 dynamic_slice.14
  29.7 44.7 %collective-permute-done = bf16[2,512,1024]{1,0,2:T(2,128)(2,1)} collective-permute-done((bf16[2,512,1024]{1,0,2:T(2,128)(2,1)}, bf16[2,512,1024]{1,0,2:T(2,128)(2,1)}, u32[]{:S(2)}, u32[]{:S(2)}) %collective-permute-start) | collective-permute-done | bytes 2097184 | tf_op jit(solution)/shard_map/ppermute | solution.py:10
  74.4 2.6 %broadcast_select_fusion.2 = bf16[2,256,1024]{1,0,2:T(2,128)(2,1)S(1)} fusion(pred[]{:T(512)S(6)} %eq.16, bf16[2,512,1024]{1,0,2:T(2,128)(2,1)} %fusion, s32[]{:T(128)S(6)} %select_n.95, bf16[2,512,1024]{1,0,2:T(2,128)(2,1)} %collective-permute-done), kind=kLoop, calls=%fused_computation.8 | loop fusion | flops 524288 | bytes 3145733 | tf_op jit(solution)/shard_map/jit(_where)/select_n | solution.py:41
  77.0 5.4 %all_to_all.15 = bf16[2,256,1024]{1,0,2:T(2,128)(2,1)} all-to-all(bf16[2,256,1024]{1,0,2:T(2,128)(2,1)S(1)} %broadcast_select_fusion.2), channel_id=1, replica_groups=mesh['gx'=8,'gy'=2,'pa'=2] {'pa'}, dimensions={2} | all-to-all | bytes 2097152 | tf_op jit(solution)/shard_map/all_to_all | solution.py:43
  82.4 2.4 %copy.10 = bf16[2,256,2,512]{3,1,2,0:T(8,128)(2,1)S(1)} copy(bf16[2,256,2,512]{1,0,3,2:T(2,128)(2,1)} %bitcast.105) | data formatting | bytes 2097152 | tf_op jit(solution)/shard_map/all_to_all | solution.py:43
  84.9 1.0 fusion.22
  85.9 4.9 %broadcast_select_fusion.1 = bf16[2,512,1024]{1,0,2:T(2,128)(2,1)S(1)} fusion(bf16[2,512,1024]{1,0,2:T(2,128)(2,1)} %collective-permute-done, pred[]{:T(512)S(6)} %eq.16, bf16[1024,2,512]{2,1,0:T(2,128)(2,1)S(1)} %gather_fusion, pred[1024]{0:T(1024)(128)(4,1)S(1)} %compare_and_fusion), kind=kLoop, calls=%fused_computation.3 | loop fusion | flops 2097152 | bytes 6292481 | tf_op jit(solution)/shard_map/jit(_where)/select_n | solution.py:40
  90.8 3.8 %fusion.21 = (bf16[1,512,1024]{1,0,2:T(2,128)(2,1)}, bf16[1,512,1024]{1,0,2:T(2,128)(2,1)S(1)}) fusion(bf16[2,512,1024]{1,0,2:T(2,128)(2,1)S(1)} %broadcast_select_fusion.1), kind=kLoop, calls=%fused_computation.55 | loop fusion | bytes 4194304 | tf_op jit(solution)/shard_map/slice | solution.py:16
  94.7 2.6 %copy.11 = bf16[1,512,1024]{2,1,0:T(8,128)(2,1)S(1)} copy(bf16[1,512,1024]{1,0,2:T(2,128)(2,1)S(1)} %get-tuple-element.5) | data formatting | bytes 2097152 | tf_op jit(solution)/shard_map/slice | solution.py:15
  97.3 4.6 %copy.12 = bf16[1,512,1024]{2,1,0:T(8,128)(2,1)S(1)} copy(bf16[1,512,1024]{1,0,2:T(2,128)(2,1)} %get-tuple-element.4) | data formatting | bytes 2097152 | tf_op jit(solution)/shard_map/slice | solution.py:16
  101.9 0.7 fusion.16
  102.7 0.7 fusion.14
  103.4 0.3 copy-done.2
  103.7 0.7 convolution_add_fusion
  104.4 0.7 convolution_subtract_fusion
  105.1 2.5 %pad_maximum_fusion = f32[512,2048]{1,0:T(8,128)} fusion(f32[512,1024]{1,0:T(8,128)S(1)} %convolution_add_fusion, f32[512,1024]{1,0:T(8,128)S(1)} %convolution_subtract_fusion), kind=kLoop, calls=%fused_computation.1 | loop fusion | flops 1048576 | bytes 8388608 | tf_op jit(solution)/shard_map/concatenate | solution.py:46
  107.7 14.7 %reduce-scatter.2.cloned.1.call-done = f32[256,2048]{1,0:T(8,128)} async-done(((f32[512,2048]{1,0:T(8,128)}), f32[256,2048]{1,0:T(8,128)}) %reduce-scatter.2.cloned.1.call-update) | async-done | bytes 2097168 | tf_op jit(solution)/shard_map/reduce_scatter | solution.py:45
  122.3 1.7 convert.20
  124.2 0.1 pad_maximum_fusion.2
  124.3 1.9 collective-permute-start.1
  126.2 0.6 constant_dynamic-slice_fusion
  127.4 22.3 %collective-permute-done.1 = bf16[2,256,1024]{2,1,0:T(8,128)(2,1)S(1)} collective-permute-done((bf16[2,256,1024]{2,1,0:T(8,128)(2,1)S(1)}, bf16[2,256,1024]{2,1,0:T(8,128)(2,1)S(1)}, u32[]{:S(2)}, u32[]{:S(2)}) %collective-permute-start.1) | collective-permute-done | bytes 1048608 | tf_op jit(solution)/shard_map/ppermute | solution.py:10
  149.7 0.1 broadcast_select_fusion.5
  149.9 1.8 collective-permute-start.2
  151.6 23.0 %collective-permute-done.2 = bf16[2,256,1024]{2,1,0:T(8,128)(2,1)} collective-permute-done((bf16[2,256,1024]{2,1,0:T(8,128)(2,1)S(1)}, bf16[2,256,1024]{2,1,0:T(8,128)(2,1)}, u32[]{:S(2)}, u32[]{:S(2)}) %collective-permute-start.2) | collective-permute-done | bytes 1048608 | tf_op jit(solution)/shard_map/ppermute | solution.py:10
  174.6 1.5 broadcast_select_fusion.4
  176.1 1.5 pad_maximum_fusion.1
  177.6 0.7 copy-done.4
  178.3 1.5 collective-permute-start.3
  179.8 2.1 %collective-permute-done.3 = f32[2,1024]{1,0:T(2,128)S(1)} collective-permute-done((f32[2,1024]{1,0:T(2,128)S(1)}, f32[2,1024]{1,0:T(2,128)S(1)}, u32[]{:S(2)}, u32[]{:S(2)}) %collective-permute-start.3) | collective-permute-done | bytes 8224 | tf_op jit(solution)/shard_map/ppermute | solution.py:10
  182.0 1.5 collective-permute-start.4
  183.5 2.1 %collective-permute-done.4 = f32[2,1024]{1,0:T(2,128)S(1)} collective-permute-done((f32[2,1024]{1,0:T(2,128)S(1)}, f32[2,1024]{1,0:T(2,128)S(1)}, u32[]{:S(2)}, u32[]{:S(2)}) %collective-permute-start.4) | collective-permute-done | bytes 8224 | tf_op jit(solution)/shard_map/ppermute | solution.py:10
  185.6 0.2 fusion.20
  185.8 6.5 %all-gather.2.cloned.1.call-done = bf16[2,1024,1024]{2,1,0:T(8,128)(2,1)} async-done(((bf16[2,512,1024]{2,1,0:T(8,128)(2,1)}), bf16[2,1024,1024]{2,1,0:T(8,128)(2,1)}) %all-gather.2.cloned.1.call-update) | async-done | bytes 4194320 | tf_op jit(solution)/shard_map/all_gather | solution.py:60
  192.4 2.2 %fusion.1 = f32[128,1024]{1,0:T(8,128)S(1)} fusion(bf16[2,1024,1024]{2,1,0:T(8,128)(2,1)} %all-gather.2.cloned.1.call-done, bf16[2,128,1024]{2,1,0:T(8,128)(2,1)S(1)} %fusion.20), kind=kOutput, calls=%fused_computation.9 | convolution fusion | flops 268435456 | bytes 2883584 | tf_op jit(solution)/shard_map/dot_general | solution.py:19
  194.6 2.1 fusion.8
  196.6 0.3 convolution_bitcast_fusion
  196.9 0.3 convolution_bitcast_fusion.2
  197.3 0.5 fusion.4
  197.8 0.5 fusion.7
  198.2 0.2 fusion.10
  198.4 0.4 fusion.12
  198.8 0.9 pad_maximum_fusion.3
  199.7 0.6 maximum_bitcast_fusion
  (22 shorter events, 0.3 us)
Async XLA Ops:
  7.2 119.0 %copy-start = (s32[4,1]{0,1:T(1,128)S(1)}, s32[4,1]{0,1:T(1,128)}, u32[]{:S(2)}) copy-start(s32[4,1]{0,1:T(1,128)} %param.8) | copy-start | bytes 52
  7.2 6.2 %copy-start.3 = (s32[1,1,1024]{2,1,0:T(1,128)S(1)}, s32[1,1,1024]{2,1,0:T(1,128)}, u32[]{:S(2)}) copy-start(s32[1,1,1024]{2,1,0:T(1,128)} %param.6) | copy-start | bytes 12292
  7.2 115.2 %reduce-scatter.2.cloned.1.call-start = ((), (), s32[]{:S(2)}) async-start(), calls=%async_computation.2 | async-start | bytes 6291456 | tf_op jit(solution)/shard_map/reduce_scatter | solution.py:45
  20.9 7.6 %copy-start.5 = (s32[4,2]{0,1:T(2,128)S(1)}, s32[4,2]{0,1:T(2,128)}, u32[]{:S(2)}) copy-start(s32[4,2]{0,1:T(2,128)} %param.7) | copy-start | bytes 100
  25.5 48.9 %collective-permute-start = (bf16[2,512,1024]{1,0,2:T(2,128)(2,1)}, bf16[2,512,1024]{1,0,2:T(2,128)(2,1)}, u32[]{:S(2)}, u32[]{:S(2)}) collective-permute-start(bf16[2,512,1024]{1,0,2:T(2,128)(2,1)} %fusion), channel_id=1, source_target_pairs={{0,4},{4,0},{8,12},{12,8},{16,20},{20,16},{24,28},{28,24},{1,5},{5... | collective-permute-start | bytes 6291464 | tf_op jit(solution)/shard_map/ppermute | solution.py:10
  97.3 4.6 %copy-start.1 = (bf16[1,2,256,512]{3,2,1,0:T(8,128)(2,1)S(1)}, bf16[1,2,256,512]{3,2,1,0:T(8,128)(2,1)}, u32[]{:S(2)}) copy-start(bf16[1,2,256,512]{3,2,1,0:T(8,128)(2,1)} %get-tuple-element.9) | copy-start | bytes 1572868
  102.6 1.0 copy-start.2
  107.6 84.8 %all-gather.2.cloned.1.call-start = ((), (), s32[]{:S(2)}) async-start(), calls=%async_computation.3 | async-start | bytes 6291456 | tf_op jit(solution)/shard_map/all_gather | solution.py:60
  124.3 25.5 %collective-permute-start.1 = (bf16[2,256,1024]{2,1,0:T(8,128)(2,1)S(1)}, bf16[2,256,1024]{2,1,0:T(8,128)(2,1)S(1)}, u32[]{:S(2)}, u32[]{:S(2)}) collective-permute-start(bf16[2,256,1024]{2,1,0:T(8,128)(2,1)S(1)} %pad_maximum_fusion.2), channel_id=1, source_target_pairs={{0,2},{2,0},{1,3},{3,1},{4,6},{6,4},{5,7},{7,5},{8,10},{10,8},{9,1... | collective-permute-start | bytes 3145736 | tf_op jit(solution)/shard_map/ppermute | solution.py:10
  149.9 24.7 %collective-permute-start.2 = (bf16[2,256,1024]{2,1,0:T(8,128)(2,1)S(1)}, bf16[2,256,1024]{2,1,0:T(8,128)(2,1)}, u32[]{:S(2)}, u32[]{:S(2)}) collective-permute-start(bf16[2,256,1024]{2,1,0:T(8,128)(2,1)S(1)} %broadcast_select_fusion.5), channel_id=1, source_target_pairs={{0,4},{4,0},{8,12},{12,8},{16,20},{20,16},{24,28},{28,24},{1,5},{5... | collective-permute-start | bytes 3145736 | tf_op jit(solution)/shard_map/ppermute | solution.py:10
  177.6 0.7 copy-start.4
  178.3 3.7 %collective-permute-start.3 = (f32[2,1024]{1,0:T(2,128)S(1)}, f32[2,1024]{1,0:T(2,128)S(1)}, u32[]{:S(2)}, u32[]{:S(2)}) collective-permute-start(f32[2,1024]{1,0:T(2,128)S(1)} %bitcast.110), channel_id=1, source_target_pairs={{0,4},{4,0},{8,12},{12,8},{16,20},{20,16},{24,28},{28,24},{1,5},{5... | collective-permute-start | bytes 24584 | tf_op jit(solution)/shard_map/ppermute | solution.py:10
  182.0 3.7 %collective-permute-start.4 = (f32[2,1024]{1,0:T(2,128)S(1)}, f32[2,1024]{1,0:T(2,128)S(1)}, u32[]{:S(2)}, u32[]{:S(2)}) collective-permute-start(f32[2,1024]{1,0:T(2,128)S(1)} %bitcast_add_fusion), channel_id=1, source_target_pairs={{0,2},{2,0},{1,3},{3,1},{4,6},{6,4},{5,7},{7,5},{8,10},{10,8},{9,1... | collective-permute-start | bytes 24584 | tf_op jit(solution)/shard_map/ppermute | solution.py:10
  192.4 4.9 %copy-start.6 = (bf16[2,1024,1024]{2,1,0:T(8,128)(2,1)S(1)}, bf16[2,1024,1024]{2,1,0:T(8,128)(2,1)}, u32[]{:S(2)}) copy-start(bf16[2,1024,1024]{2,1,0:T(8,128)(2,1)} %all-gather.2.cloned.1.call-done) | copy-start | bytes 12582916
Sparse Core Ops, SparseCore 0:
  107.7 14.5 reduce-scatter.1
  177.8 14.5 all-gather.1
where the time goes:
time: 208 us; the launch traced here: 207 us
  waiting for transfers between devices  115 us (55%)
  local copies, waits for them, and re-layouts  30.4 us (15%)
  other arithmetic  21.2 us (10%)
  between operations  15.6 us (8%)
  starting transfers between devices  9.77 us (5%)
  matrix products  9.28 us (4%)
  blocking collectives  5.37 us (3%)
    ppermute x5, waiting for transfers between devices, from_partner(): return lax.ppermute(value, axis, pairs)  94.2 us
    reduce_scatter x1, waiting for transfers between devices, per_device(): lax.psum_scatter(jnp.concatenate([real_part, imag_part], axis=1), 'pa', s...  14.7 us
    ppermute x5, starting transfers between devices, from_partner(): return lax.ppermute(value, axis, pairs)  9.69 us
    slice x2, local copies, waits for them, and re-layouts, complex_rows(): right_block[1]  8.47 us
    gather x1, local copies, waits for them, and re-layouts, per_device(): own_panel = jnp.take(leaf_maps[0, 0], face_index[0, 0], axis=2)  7.46 us
    unnamed x15, local copies, waits for them, and re-layouts  7.18 us
    all_gather x1, waiting for transfers between devices, per_device(): lax.all_gather(full_panel, 'pa', axis=1, tiled=True)  6.54 us
    all_to_all x1, blocking collectives, per_device(): lax.all_to_all(left_rows, 'pa', split_axis=2, concat_axis=1, tiled=True)  5.37 us
  transfers between devices with their start and end apart: 7, of which 7 were waited for; matrix products, arithmetic and copies ran while one was open for 1% of the time, Pallas kernels for 0%

commit v1 on v0

--- a/solution.py
+++ b/solution.py
@@ -40,7 +40,10 @@
     right_panel = jnp.where(half_index == first_bit, own_panel, sibling)
     left_panel = jnp.where(half_index == first_bit, sibling, own_panel)
     left_rows = lax.dynamic_slice_in_dim(left_panel, half_index * half_rows, half_rows, 1)
-    blocks = lax.all_to_all(left_rows, "pa", split_axis=2, concat_axis=1, tiled=True)
+    blocks = jnp.concatenate(
+        lax.all_to_all(jnp.stack(jnp.split(left_rows, lax.axis_size("pa"), axis=2)), "pa", 0, 0),
+        axis=1,
+    )
     real_part, imag_part = complex_rows(blocks, right_panel)
     summed = lax.psum_scatter(
         jnp.concatenate([real_part, imag_part], axis=1), "pa", scatter_dimension=0, tiled=True

time: 208 us -> 212 us (1.019)
  local copies, waits for them, and re-layouts: 30.4 us -> 34.3 us
    slice x1 -> x2, local copies, waits for them, and re-layouts: 1.04 us -> 4.67 us  [complex_rows(): left_block[0]]
    all_to_all x1 -> x0, local copies, waits for them, and re-layouts: 2.45 us -> none  [per_device(): lax.all_to_all(left_rows, 'pa', split_axis=2, concat_axis=1, tiled=True)]
    slice x0 -> x1, local copies, waits for them, and re-layouts: none -> 2.28 us  [complex_rows(): left_block[1]]
    unnamed x15 -> x13, local copies, waits for them, and re-layouts: 7.18 us -> 6.86 us
where the time goes in v1:
time: 212 us
  waiting for transfers between devices  115 us (54%)
  local copies, waits for them, and re-layouts  34.3 us (16%)
  other arithmetic  22.7 us (11%)
  between operations  15.6 us (7%)
  starting transfers between devices  9.95 us (5%)
  matrix products  9.29 us (4%)
  blocking collectives  4.58 us (2%)
    ppermute x5, waiting for transfers between devices, from_partner(): return lax.ppermute(value, axis, pairs)  94.2 us
    reduce_scatter x1, waiting for transfers between devices, per_device(): lax.psum_scatter(jnp.concatenate([real_part, imag_part], axis=1), 'pa', s...  14.5 us
    ppermute x5, starting transfers between devices, from_partner(): return lax.ppermute(value, axis, pairs)  9.69 us
    slice x2, local copies, waits for them, and re-layouts, complex_rows(): right_block[1]  8.41 us
    gather x1, local copies, waits for them, and re-layouts, per_device(): own_panel = jnp.take(leaf_maps[0, 0], face_index[0, 0], axis=2)  7.46 us
    unnamed x13, local copies, waits for them, and re-layouts  6.86 us
    all_gather x1, waiting for transfers between devices, per_device(): lax.all_gather(full_panel, 'pa', axis=1, tiled=True)  6.54 us
    select_n x1, other arithmetic, per_device(): right_panel = jnp.where(half_index == first_bit, own_panel, sibling)  4.9 us
  transfers between devices with their start and end apart: 7, of which 7 were waited for; matrix products, arithmetic and copies ran while one was open for 1% of the time, Pallas kernels for 0%

profile of v1, /device:TPU:0, one launch (start us, length us, event | category | flops | bytes accessed | tf_op | source)
XLA Modules:
  0.0 211.6 jit_solution(275536771545331185)
XLA Ops:
  7.2 6.2 %copy.8 = bf16[1,1,2,512,1024]{3,2,4,1,0:T(2,128)(2,1)} copy(bf16[1,1,2,512,1024]{4,3,2,1,0:T(8,128)(2,1)} %param.5) | data formatting | bytes 4194304 | tf_op args[0]
  13.4 7.5 %gather_fusion = bf16[1024,2,512]{2,1,0:T(2,128)(2,1)S(1)} fusion(bf16[2,512,1024]{1,0,2:T(2,128)(2,1)} %bitcast.103, s32[1024]{0:T(1024)S(1)} %broadcast_clamp_fusion), kind=kCustom, calls=%fused_computation | custom fusion | bytes 4198400 | tf_op jit(solution)/shard_map/jit(_take)/gather | solution.py:29
  20.9 4.6 %fusion = bf16[2,512,1024]{1,0,2:T(2,128)(2,1)} fusion(bf16[1024,2,512]{2,1,0:T(2,128)(2,1)S(1)} %gather_fusion, pred[1024]{0:T(1024)(128)(4,1)S(1)} %compare_and_fusion), kind=kLoop, calls=%fused_computation.7 | loop fusion | flops 1048576 | bytes 4195328 | tf_op jit(solution)/shard_map/jit(_take)/select_n | solution.py:29
  25.5 3.0 %collective-permute-start = (bf16[2,512,1024]{1,0,2:T(2,128)(2,1)}, bf16[2,512,1024]{1,0,2:T(2,128)(2,1)}, u32[]{:S(2)}, u32[]{:S(2)}) collective-permute-start(bf16[2,512,1024]{1,0,2:T(2,128)(2,1)} %fusion), channel_id=1, source_target_pairs={{0,4},{4,0},{8,12},{12,8},{16,20},{20,16},{24,28},{28,24},{1,5},{5... | collective-permute-start | bytes 6291464 | tf_op jit(solution)/shard_map/ppermute | solution.py:10
  28.5 0.6 dynamic_slice.14
  29.7 44.7 %collective-permute-done = bf16[2,512,1024]{1,0,2:T(2,128)(2,1)} collective-permute-done((bf16[2,512,1024]{1,0,2:T(2,128)(2,1)}, bf16[2,512,1024]{1,0,2:T(2,128)(2,1)}, u32[]{:S(2)}, u32[]{:S(2)}) %collective-permute-start) | collective-permute-done | bytes 2097184 | tf_op jit(solution)/shard_map/ppermute | solution.py:10
  74.4 2.6 %broadcast_select_fusion.2 = bf16[2,256,1024]{1,0,2:T(2,128)(2,1)S(1)} fusion(pred[]{:T(512)S(6)} %eq.16, bf16[2,512,1024]{1,0,2:T(2,128)(2,1)} %fusion, s32[]{:T(128)S(6)} %select_n.95, bf16[2,512,1024]{1,0,2:T(2,128)(2,1)} %collective-permute-done), kind=kLoop, calls=%fused_computation.8 | loop fusion | flops 524288 | bytes 3145733 | tf_op jit(solution)/shard_map/jit(_where)/select_n | solution.py:41
  77.0 0.7 slice_bitcast_fusion.17
  77.8 1.5 pad_maximum_fusion.3
  79.3 4.6 %all_to_all.5 = bf16[2,2,256,512]{2,1,3,0:T(2,128)(2,1)S(1)} all-to-all(bf16[2,2,256,512]{2,1,3,0:T(2,128)(2,1)S(1)} %pad_maximum_fusion.3), channel_id=1, replica_groups=mesh['gx'=8,'gy'=2,'pa'=2] {'pa'}, dimensions={0} | all-to-all | bytes 2097152 | tf_op jit(solution)/shard_map/all_to_all | solution.py:44
  83.8 2.3 %fusion.22 = (bf16[1,2,256,512]{2,0,3,1:T(2,128)(2,1)}, bf16[1,2,256,512]{2,0,3,1:T(2,128)(2,1)S(1)}) fusion(bf16[2,2,256,512]{2,0,3,1:T(2,128)(2,1)S(1)} %bitcast.102), kind=kLoop, calls=%fused_computation.59 | loop fusion | bytes 2097152 | tf_op jit(solution)/shard_map/slice | solution.py:15
  86.1 2.3 %copy.11 = bf16[1,2,256,512]{3,2,1,0:T(8,128)(2,1)} copy(bf16[1,2,256,512]{2,0,3,1:T(2,128)(2,1)S(1)} %get-tuple-element.9) | data formatting | bytes 1048576 | tf_op jit(solution)/shard_map/slice | solution.py:16
  88.4 4.9 %broadcast_select_fusion.1 = bf16[2,512,1024]{1,0,2:T(2,128)(2,1)S(1)} fusion(bf16[2,512,1024]{1,0,2:T(2,128)(2,1)} %collective-permute-done, pred[]{:T(512)S(6)} %eq.16, bf16[1024,2,512]{2,1,0:T(2,128)(2,1)S(1)} %gather_fusion, pred[1024]{0:T(1024)(128)(4,1)S(1)} %compare_and_fusion), kind=kLoop, calls=%fused_computation.3 | loop fusion | flops 2097152 | bytes 6292481 | tf_op jit(solution)/shard_map/jit(_where)/select_n | solution.py:40
  93.3 3.8 %fusion.21 = (bf16[1,512,1024]{1,0,2:T(2,128)(2,1)}, bf16[1,512,1024]{1,0,2:T(2,128)(2,1)S(1)}) fusion(bf16[2,512,1024]{1,0,2:T(2,128)(2,1)S(1)} %broadcast_select_fusion.1), kind=kLoop, calls=%fused_computation.58 | loop fusion | bytes 4194304 | tf_op jit(solution)/shard_map/slice | solution.py:16
  97.1 2.6 %copy.10 = bf16[1,512,1024]{2,1,0:T(8,128)(2,1)S(1)} copy(bf16[1,512,1024]{1,0,2:T(2,128)(2,1)S(1)} %get-tuple-element.5) | data formatting | bytes 2097152 | tf_op jit(solution)/shard_map/slice | solution.py:15
  99.8 2.4 %copy.9 = bf16[1,2,256,512]{3,2,1,0:T(8,128)(2,1)S(1)} copy(bf16[1,2,256,512]{2,0,3,1:T(2,128)(2,1)} %get-tuple-element.8) | data formatting | bytes 1048576 | tf_op jit(solution)/shard_map/slice | solution.py:15
  102.2 4.6 %copy.12 = bf16[1,512,1024]{2,1,0:T(8,128)(2,1)S(1)} copy(bf16[1,512,1024]{1,0,2:T(2,128)(2,1)} %get-tuple-element.4) | data formatting | bytes 2097152 | tf_op jit(solution)/shard_map/slice | solution.py:16
  106.8 0.7 fusion.16
  107.5 0.7 fusion.14
  108.2 0.7 convolution_add_fusion
  108.9 0.7 convolution_subtract_fusion
  109.6 2.5 %pad_maximum_fusion = f32[512,2048]{1,0:T(8,128)} fusion(f32[512,1024]{1,0:T(8,128)S(1)} %convolution_add_fusion, f32[512,1024]{1,0:T(8,128)S(1)} %convolution_subtract_fusion), kind=kLoop, calls=%fused_computation.1 | loop fusion | flops 1048576 | bytes 8388608 | tf_op jit(solution)/shard_map/concatenate | solution.py:49
  112.1 0.2 all-gather.2.cloned.1.call-start
  112.3 14.5 %reduce-scatter.2.cloned.1.call-done = f32[256,2048]{1,0:T(8,128)} async-done(((f32[512,2048]{1,0:T(8,128)}), f32[256,2048]{1,0:T(8,128)}) %reduce-scatter.2.cloned.1.call-update) | async-done | bytes 2097168 | tf_op jit(solution)/shard_map/reduce_scatter | solution.py:48
  126.9 1.7 convert.20
  128.8 1.9 collective-permute-start.1
  130.7 0.6 constant_dynamic-slice_fusion
  131.9 22.3 %collective-permute-done.1 = bf16[2,256,1024]{2,1,0:T(8,128)(2,1)S(1)} collective-permute-done((bf16[2,256,1024]{2,1,0:T(8,128)(2,1)S(1)}, bf16[2,256,1024]{2,1,0:T(8,128)(2,1)S(1)}, u32[]{:S(2)}, u32[]{:S(2)}) %collective-permute-start.1) | collective-permute-done | bytes 1048608 | tf_op jit(solution)/shard_map/ppermute | solution.py:10
  154.4 1.8 collective-permute-start.2
  156.1 23.0 %collective-permute-done.2 = bf16[2,256,1024]{2,1,0:T(8,128)(2,1)} collective-permute-done((bf16[2,256,1024]{2,1,0:T(8,128)(2,1)S(1)}, bf16[2,256,1024]{2,1,0:T(8,128)(2,1)}, u32[]{:S(2)}, u32[]{:S(2)}) %collective-permute-start.2) | collective-permute-done | bytes 1048608 | tf_op jit(solution)/shard_map/ppermute | solution.py:10
  179.1 1.5 broadcast_select_fusion.4
  180.6 1.5 pad_maximum_fusion.1
  182.1 0.7 copy-done.3
  182.8 1.5 collective-permute-start.3
  184.3 2.1 %collective-permute-done.3 = f32[2,1024]{1,0:T(2,128)S(1)} collective-permute-done((f32[2,1024]{1,0:T(2,128)S(1)}, f32[2,1024]{1,0:T(2,128)S(1)}, u32[]{:S(2)}, u32[]{:S(2)}) %collective-permute-start.3) | collective-permute-done | bytes 8224 | tf_op jit(solution)/shard_map/ppermute | solution.py:10
  186.5 1.5 collective-permute-start.4
  188.0 2.1 %collective-permute-done.4 = f32[2,1024]{1,0:T(2,128)S(1)} collective-permute-done((f32[2,1024]{1,0:T(2,128)S(1)}, f32[2,1024]{1,0:T(2,128)S(1)}, u32[]{:S(2)}, u32[]{:S(2)}) %collective-permute-start.4) | collective-permute-done | bytes 8224 | tf_op jit(solution)/shard_map/ppermute | solution.py:10
  190.3 6.5 %all-gather.2.cloned.1.call-done = bf16[2,1024,1024]{2,1,0:T(8,128)(2,1)} async-done(((bf16[2,512,1024]{2,1,0:T(8,128)(2,1)}), bf16[2,1024,1024]{2,1,0:T(8,128)(2,1)}) %all-gather.2.cloned.1.call-update) | async-done | bytes 4194320 | tf_op jit(solution)/shard_map/all_gather | solution.py:63
  196.9 2.2 %fusion.1 = f32[128,1024]{1,0:T(8,128)S(1)} fusion(bf16[2,1024,1024]{2,1,0:T(8,128)(2,1)} %all-gather.2.cloned.1.call-done, bf16[2,128,1024]{2,1,0:T(8,128)(2,1)S(1)} %fusion.20), kind=kOutput, calls=%fused_computation.9 | convolution fusion | flops 268435456 | bytes 2883584 | tf_op jit(solution)/shard_map/dot_general | solution.py:19
  199.1 2.1 fusion.8
  201.2 0.3 convolution_bitcast_fusion
  201.5 0.3 convolution_bitcast_fusion.2
  201.8 0.5 fusion.4
  202.3 0.5 fusion.7
  202.7 0.2 fusion.10
  203.0 0.4 fusion.12
  203.4 0.9 pad_maximum_fusion.4
  204.2 0.6 maximum_bitcast_fusion
  (23 shorter events, 0.6 us)
Async XLA Ops:
  7.2 123.5 %copy-start = (s32[4,1]{0,1:T(1,128)S(1)}, s32[4,1]{0,1:T(1,128)}, u32[]{:S(2)}) copy-start(s32[4,1]{0,1:T(1,128)} %param.8) | copy-start | bytes 52
  7.2 6.2 %copy-start.2 = (s32[1,1,1024]{2,1,0:T(1,128)S(1)}, s32[1,1,1024]{2,1,0:T(1,128)}, u32[]{:S(2)}) copy-start(s32[1,1,1024]{2,1,0:T(1,128)} %param.6) | copy-start | bytes 12292
  7.2 119.7 %reduce-scatter.2.cloned.1.call-start = ((), (), s32[]{:S(2)}) async-start(), calls=%async_computation.2 | async-start | bytes 6291456 | tf_op jit(solution)/shard_map/reduce_scatter | solution.py:48
  20.9 7.6 %copy-start.4 = (s32[4,2]{0,1:T(2,128)S(1)}, s32[4,2]{0,1:T(2,128)}, u32[]{:S(2)}) copy-start(s32[4,2]{0,1:T(2,128)} %param.7) | copy-start | bytes 100
  25.5 48.9 %collective-permute-start = (bf16[2,512,1024]{1,0,2:T(2,128)(2,1)}, bf16[2,512,1024]{1,0,2:T(2,128)(2,1)}, u32[]{:S(2)}, u32[]{:S(2)}) collective-permute-start(bf16[2,512,1024]{1,0,2:T(2,128)(2,1)} %fusion), channel_id=1, source_target_pairs={{0,4},{4,0},{8,12},{12,8},{16,20},{20,16},{24,28},{28,24},{1,5},{5... | collective-permute-start | bytes 6291464 | tf_op jit(solution)/shard_map/ppermute | solution.py:10
  99.7 7.0 %copy-start.1 = (bf16[1,2,256,512]{3,2,1,0:T(8,128)(2,1)S(1)}, bf16[1,2,256,512]{3,2,1,0:T(8,128)(2,1)}, u32[]{:S(2)}) copy-start(bf16[1,2,256,512]{3,2,1,0:T(8,128)(2,1)} %copy.11) | copy-start | bytes 1572868
  112.1 84.8 %all-gather.2.cloned.1.call-start = ((), (), s32[]{:S(2)}) async-start(), calls=%async_computation.3 | async-start | bytes 6291456 | tf_op jit(solution)/shard_map/all_gather | solution.py:63
  128.8 25.5 %collective-permute-start.1 = (bf16[2,256,1024]{2,1,0:T(8,128)(2,1)S(1)}, bf16[2,256,1024]{2,1,0:T(8,128)(2,1)S(1)}, u32[]{:S(2)}, u32[]{:S(2)}) collective-permute-start(bf16[2,256,1024]{2,1,0:T(8,128)(2,1)S(1)} %pad_maximum_fusion.2), channel_id=1, source_target_pairs={{0,2},{2,0},{1,3},{3,1},{4,6},{6,4},{5,7},{7,5},{8,10},{10,8},{9,1... | collective-permute-start | bytes 3145736 | tf_op jit(solution)/shard_map/ppermute | solution.py:10
  154.4 24.7 %collective-permute-start.2 = (bf16[2,256,1024]{2,1,0:T(8,128)(2,1)S(1)}, bf16[2,256,1024]{2,1,0:T(8,128)(2,1)}, u32[]{:S(2)}, u32[]{:S(2)}) collective-permute-start(bf16[2,256,1024]{2,1,0:T(8,128)(2,1)S(1)} %broadcast_select_fusion.5), channel_id=1, source_target_pairs={{0,4},{4,0},{8,12},{12,8},{16,20},{20,16},{24,28},{28,24},{1,5},{5... | collective-permute-start | bytes 3145736 | tf_op jit(solution)/shard_map/ppermute | solution.py:10
  182.1 0.7 copy-start.3
  182.8 3.7 %collective-permute-start.3 = (f32[2,1024]{1,0:T(2,128)S(1)}, f32[2,1024]{1,0:T(2,128)S(1)}, u32[]{:S(2)}, u32[]{:S(2)}) collective-permute-start(f32[2,1024]{1,0:T(2,128)S(1)} %bitcast.112), channel_id=1, source_target_pairs={{0,4},{4,0},{8,12},{12,8},{16,20},{20,16},{24,28},{28,24},{1,5},{5... | collective-permute-start | bytes 24584 | tf_op jit(solution)/shard_map/ppermute | solution.py:10
  186.5 3.7 %collective-permute-start.4 = (f32[2,1024]{1,0:T(2,128)S(1)}, f32[2,1024]{1,0:T(2,128)S(1)}, u32[]{:S(2)}, u32[]{:S(2)}) collective-permute-start(f32[2,1024]{1,0:T(2,128)S(1)} %bitcast_add_fusion), channel_id=1, source_target_pairs={{0,2},{2,0},{1,3},{3,1},{4,6},{6,4},{5,7},{7,5},{8,10},{10,8},{9,1... | collective-permute-start | bytes 24584 | tf_op jit(solution)/shard_map/ppermute | solution.py:10
  196.9 4.9 %copy-start.5 = (bf16[2,1024,1024]{2,1,0:T(8,128)(2,1)S(1)}, bf16[2,1024,1024]{2,1,0:T(8,128)(2,1)}, u32[]{:S(2)}) copy-start(bf16[2,1024,1024]{2,1,0:T(8,128)(2,1)} %all-gather.2.cloned.1.call-done) | copy-start | bytes 12582916
Sparse Core Ops, SparseCore 0:
  112.2 14.5 reduce-scatter.1
  182.3 14.5 all-gather.1
